TPU v7x, 128 devices: a whole 4x4x4 slice. The times are simulated.
128 devices in a mesh: row: 4 (over y), col: 4 (over x_hi, core), chol: 8 (over z, x_lo).
Axes of the slice: x: 4 (x_hi: 2, x_lo: 2; x = x_hi * 2 + x_lo), y: 4, z: 4, core: 2. Of those that a mesh axis runs over, the one named last changes fastest.
Arguments:
- left_vectors: bfloat16 [64, 4608, 1536], P(None, ('col', 'chol'), 'row'), may hold values from -0.75 to 0.75
- right_vectors: bfloat16 [16, 4608, 1536], P(None, ('col', 'chol'), 'row'), may hold values from -0.0234375 to 0.0234375
- amplitudes: bfloat16 [8, 16, 64], replicated, may hold values from -6 to 6
Outputs:
- ladder: float32 [8, 1536, 1536], P('chol', 'row', 'col')
All inputs are finite; a program needn't handle non-finite values.
Results may differ from a plain program's by a relative error of at most 0.0029.
Values may be sent and summed in bfloat16 or wider, within the bound.
A program may use at most 128 MiB of HBM per device.

v0:
```python
import jax
import jax.numpy as jnp
from jax import lax
from jax.sharding import Mesh
from jax.sharding import PartitionSpec as P

COL = ("col_0", "col_1")
COL_CHOL = ("col_0", "col_1", "chol_0", "chol_1")
CHOL = ("chol_0", "chol_1")


def reduced_to_own(parts, axes, order):
    inside = parts.shape[1:]
    parts = parts.reshape(*(lax.axis_size(a) for a in axes), *inside)
    parts = jnp.moveaxis(parts, order, range(len(axes))).reshape(-1, *inside)
    for k in order:
        parts = lax.psum_scatter(parts, axes[k], scatter_dimension=0, tiled=True)
    return parts[0]


def split_up(array, dim, devices):
    before, after = (array.shape[:dim], array.shape[dim + 1 :])
    return jnp.moveaxis(array.reshape(*before, devices, -1, *after), dim, 0)


def sum_by_axis(array, axes, order, dim):
    devices = lax.axis_size(axes)
    return reduced_to_own(split_up(array, dim, devices), axes, order)


def shards(left_vectors, right_vectors, amplitudes):
    pairs, d_block, c_block = amplitudes.shape
    amp_rows = amplitudes.reshape(pairs * d_block, c_block)
    width_a = left_vectors.shape[2]
    right_full = lax.all_gather(right_vectors, "row", axis=2, tiled=True)
    columns = lax.axis_size(COL)
    width_b = right_full.shape[2] // columns
    vectors = left_vectors.shape[1]
    halved = jnp.dot(
        amp_rows,
        left_vectors.reshape(c_block, vectors * width_a),
        preferred_element_type=jnp.float32,
    ).astype(jnp.bfloat16)
    halved = halved.reshape(pairs, d_block * vectors, width_a)
    panel = right_full.reshape(d_block * vectors, columns, width_b)
    ladder = jnp.einsum("ika,kcb->ciab", halved, panel, preferred_element_type=jnp.float32)
    ladder = ladder.reshape(columns * pairs, width_a, width_b)
    return sum_by_axis(ladder, COL_CHOL, (1, 2, 3, 0), 0)


def solution(mesh):
    finer = Mesh(
        mesh.devices.reshape(mesh.shape["row"], 2, 2, 4, 2),
        ("row", "col_0", "col_1", "chol_0", "chol_1"),
    )
    placed = (P(None, COL_CHOL, "row"), P(None, COL_CHOL, "row"), P())
    return jax.shard_map(
        shards, mesh=finer, in_specs=placed, out_specs=P(CHOL, "row", COL), check_vma=False
    )
```

profile of v0, /device:TPU:1, one launch (start us, length us, event | category | flops | bytes accessed | tf_op | source)
XLA Modules:
  0.0 329.1 jit_solution(12678364992241984205)
XLA Ops:
  6.5 0.0 copy-start
  6.5 0.0 all-gather.2.cloned.1.call-start
  6.5 0.7 all-gather.2.cloned.1.call-update
  7.3 0.0 reduce-scatter.5.cloned.1.call-start
  7.3 7.5 %copy.12 = bf16[8,8,144,384]{3,1,2,0:T(8,128)(2,1)} copy(bf16[8,8,144,384]{3,2,1,0:T(8,128)(2,1)} %bitcast.24) | data formatting | bytes 14155776
  14.8 0.0 copy-done
  14.8 11.0 %convolution_convert_fusion = bf16[128,55296]{1,0:T(8,128)(2,1)} fusion(bf16[128,64]{1,0:T(8,128)(2,1)S(1)} %bitcast.20, bf16[64,55296]{1,0:T(8,128)(2,1)} %bitcast.22), kind=kOutput, calls=%fused_computation | convolution fusion | flops 913047552 | bytes 21250048 | tf_op jit(solution)/shard_map/dot_general | solution.py:39
  25.8 18.5 %reshape.17 = bf16[8,2304,384]{2,1,0:T(8,128)(2,1)} reshape(bf16[128,55296]{1,0:T(8,128)(2,1)} %convolution_convert_fusion) | data formatting | bytes 28311552 | tf_op jit(solution)/shard_map/reshape | solution.py:44
  44.3 39.9 %all-gather.2.cloned.1.call-done = bf16[16,144,1536]{2,1,0:T(8,128)(2,1)} async-done(((bf16[16,144,384]{2,1,0:T(8,128)(2,1)}), bf16[16,144,1536]{2,1,0:T(8,128)(2,1)}) %all-gather.2.cloned.1.call-update) | async-done | bytes 7077904 | tf_op jit(solution)/shard_map/all_gather | solution.py:35
  84.3 12.7 %reshape.18 = bf16[2304,4,384]{2,1,0:T(4,128)(2,1)} reshape(bf16[16,144,1536]{2,1,0:T(8,128)(2,1)} %all-gather.2.cloned.1.call-done) | data formatting | bytes 14155776 | tf_op jit(solution)/shard_map/reshape | solution.py:45
  97.0 27.2 %fusion = f32[8,384,4,384]{3,1,2,0:T(8,128)S(1)} fusion(bf16[8,2304,384]{2,1,0:T(8,128)(2,1)} %reshape.17, bf16[2304,4,384]{2,1,0:T(4,128)(2,1)} %reshape.18), kind=kOutput, calls=%fused_computation.1 | convolution fusion | flops 21743271936 | bytes 40108032 | tf_op jit(solution)/shard_map/ika,kcb->ciab/dot_general | solution.py:46
  124.2 6.8 %copy.8 = f32[2,4,2,2,1,384,384]{6,5,3,2,1,0,4:T(8,128)} copy(f32[2,4,2,2,1,384,384]{6,5,0,3,2,1,4:T(8,128)S(1)} %bitcast.23) | data formatting | bytes 37748736 | tf_op jit(solution)/shard_map/transpose | solution.py:15
  131.0 0.0 reduce-scatter.5.cloned.1.call-update
  131.0 0.0 copy-start.1
  131.0 0.0 reduce-scatter.7.cloned.1.call-start
  131.1 30.6 %reduce-scatter.5.cloned.1.call-done = f32[16,1,384,384]{3,2,1,0:T(8,128)} async-done(((f32[32,1,384,384]{3,2,1,0:T(8,128)}), f32[16,1,384,384]{3,2,1,0:T(8,128)}) %reduce-scatter.5.cloned.1.call-update) | async-done | bytes 9437200 | tf_op jit(solution)/shard_map/reduce_scatter | solution.py:17
  161.7 0.0 reduce-scatter.7.cloned.1.call-update
  161.7 0.0 reduce-scatter.9.cloned.1.call-start
  161.8 92.7 %reduce-scatter.7.cloned.1.call-done = f32[4,1,384,384]{3,2,1,0:T(8,128)} async-done(((f32[16,1,384,384]{3,2,1,0:T(8,128)}), f32[4,1,384,384]{3,2,1,0:T(8,128)}) %reduce-scatter.7.cloned.1.call-update) | async-done | bytes 2359312 | tf_op jit(solution)/shard_map/reduce_scatter | solution.py:17
  254.5 0.0 reduce-scatter.9.cloned.1.call-update
  254.5 0.0 reduce-scatter.11.cloned.1.call-start
  254.6 38.9 %reduce-scatter.9.cloned.1.call-done = f32[2,1,384,384]{3,2,1,0:T(8,128)} async-done(((f32[4,1,384,384]{3,2,1,0:T(8,128)}), f32[2,1,384,384]{3,2,1,0:T(8,128)}) %reduce-scatter.9.cloned.1.call-update) | async-done | bytes 1179664 | tf_op jit(solution)/shard_map/reduce_scatter | solution.py:17
  293.5 0.0 reduce-scatter.11.cloned.1.call-update
  293.5 29.1 %reduce-scatter.11.cloned.1.call-done = f32[1,1,384,384]{3,2,1,0:T(8,128)} async-done(((f32[2,1,384,384]{3,2,1,0:T(8,128)}), f32[1,1,384,384]{3,2,1,0:T(8,128)}) %reduce-scatter.11.cloned.1.call-update) | async-done | bytes 589840 | tf_op jit(solution)/shard_map/reduce_scatter | solution.py:17
  322.6 0.0 copy-done.1
Async XLA Ops:
  6.5 8.3 %copy-start = (bf16[8,16,64]{2,1,0:T(8,128)(2,1)S(1)}, bf16[8,16,64]{2,1,0:T(8,128)(2,1)}, u32[]{:S(2)}) copy-start(bf16[8,16,64]{2,1,0:T(8,128)(2,1)} %param.5) | copy-start | bytes 49156
  6.5 77.7 %all-gather.2.cloned.1.call-start = ((), (), s32[]{:S(2)}) async-start(), calls=%async_computation.4 | async-start | bytes 8847360 | tf_op jit(solution)/shard_map/all_gather | solution.py:35
  7.3 154.4 %reduce-scatter.5.cloned.1.call-start = ((), (), s32[]{:S(2)}) async-start(), calls=%async_computation.5 | async-start | bytes 28311552 | tf_op jit(solution)/shard_map/reduce_scatter | solution.py:17
  131.0 191.6 %copy-start.1 = (bf16[8,16,64]{2,1,0:T(8,128)(2,1)S(1)}, bf16[8,16,64]{2,1,0:T(8,128)(2,1)}, u32[]{:S(2)}) copy-start(bf16[8,16,64]{2,1,0:T(8,128)(2,1)} %param.5) | copy-start | bytes 49156
  131.0 123.4 %reduce-scatter.7.cloned.1.call-start = ((), (), s32[]{:S(2)}) async-start(), calls=%async_computation.6 | async-start | bytes 11796480 | tf_op jit(solution)/shard_map/reduce_scatter | solution.py:17
  161.7 131.8 %reduce-scatter.9.cloned.1.call-start = ((), (), s32[]{:S(2)}) async-start(), calls=%async_computation.7 | async-start | bytes 3538944 | tf_op jit(solution)/shard_map/reduce_scatter | solution.py:17
  254.5 68.1 %reduce-scatter.11.cloned.1.call-start = ((), (), s32[]{:S(2)}) async-start(), calls=%async_computation.8 | async-start | bytes 1769472 | tf_op jit(solution)/shard_map/reduce_scatter | solution.py:17
Sparse Core Ops, SparseCore 0:
  9.0 75.2 all-gather.1
  131.1 30.5 reduce-scatter.4
  164.2 90.2 reduce-scatter.6
  256.7 36.7 reduce-scatter.8
  295.7 26.8 reduce-scatter.10
where the time goes:
time: 330 us; the launch traced here: 329 us
  waiting for transfers between devices  232 us (70%)
  local copies, waits for them, and re-layouts  45.6 us (14%)
  matrix products  38.2 us (12%)
  between operations  13.2 us (4%)
    reduce_scatter x4, waiting for transfers between devices, reduced_to_own(): parts = lax.psum_scatter(parts, axes[k], scatter_dimension=0, tiled=True)  191 us
    all_gather x1, waiting for transfers between devices, shards(): right_full = lax.all_gather(right_vectors, 'row', axis=2, tiled=True)  39.9 us
    dot_general x1, matrix products, shards(): jnp.einsum('ika,kcb->ciab', halved, panel, preferred_element_type=jnp.flo...  27.2 us
    reshape x1, local copies, waits for them, and re-layouts, shards(): halved = halved.reshape(pairs, d_block * vectors, width_a)  18.5 us
    reshape x1, local copies, waits for them, and re-layouts, shards(): panel = right_full.reshape(d_block * vectors, columns, width_b)  12.7 us
    dot_general x1, matrix products, shards(): jnp.dot(amp_rows, left_vectors.reshape(c_block, vectors * width_a), prefe...  11 us
    unnamed x5, local copies, waits for them, and re-layouts  7.54 us
    transpose x1, local copies, waits for them, and re-layouts, reduced_to_own(): parts = jnp.moveaxis(parts, order, range(len(axes))).reshape(-1, *inside)  6.82 us
  transfers between devices with their start and end apart: 5, of which 5 were waited for; matrix products, arithmetic and copies ran while one was open for 11% of the time, Pallas kernels for 0%

commit v1 on v0

v1 whole, which is shorter than its diff:
```python
import functools

import jax
import jax.numpy as jnp
from jax import lax
from jax.experimental import pallas as pl
from jax.experimental.pallas import tpu as pltpu
from jax.sharding import Mesh
from jax.sharding import PartitionSpec as P

COL = ("col_0", "col_1")
COL_CHOL = ("col_0", "col_1", "chol_0", "chol_1")
CHOL = ("chol_0", "chol_1")
MESH = pl.DeviceIdType.MESH
F32 = jnp.float32
BF16 = jnp.bfloat16
CH = 128
PB = 16

GROUPS = (
    ((0, 0), (0, 1)),
    ((0, 2),),
    ((3, 0), (1, 2)),
    ((3, 1), (1, 1)),
    ((3, 2), (1, 0)),
    ((2, 0), (2, 2)),
    ((2, 1),),
)
NG = len(GROUPS)
GATHERED = 2


def where():
    return dict(
        y=lax.axis_index("row"),
        x=lax.axis_index("col_0") * 2 + lax.axis_index("chol_1"),
        z=lax.axis_index("chol_0"),
        c=lax.axis_index("col_1"),
    )


def device(y, x, z, c):
    return (y, x // 2, c, z, lax.rem(x, 2))


def kernel(
    sizes, amp_ref, left_hbm, right_hbm, out_ref,
    left_buf, left_f32, right_buf, right_f32, own, got, halved, prod, core_got, chip, z_got,
    summed, x_got,
    load_sem, right_sem, ag_send, ag_recv, core_send, core_recv, z_send, z_recv, x_send, x_recv,
):
    pairs, d_block, c_block, vectors, width = sizes
    depth = d_block * vectors
    me = where()
    y, x, z, c = me["y"], me["x"], me["z"], me["c"]
    up = device(lax.rem(y + 1, 4), x, z, c)
    down = device(lax.rem(y + 3, 4), x, z, c)
    partner = device(y, x, z, 1 - c)

    barrier = pltpu.get_barrier_semaphore()
    others = [up, down, partner]
    others += [device(y, x, lax.rem(z + k, 4), c) for k in (1, 2, 3)]
    others += [device(y, lax.rem(x + k, 4), z, q) for k in (1, 2, 3) for q in (c, 1 - c)]
    for other in others:
        pl.semaphore_signal(barrier, inc=1, device_id=other, device_id_type=MESH)

    load_right = pltpu.make_async_copy(right_hbm, right_buf, right_sem)
    load_right.start()

    def load_left(block, slot):
        return pltpu.make_async_copy(
            left_hbm.at[:, pl.ds(pl.multiple_of(block * PB, PB), PB), :],
            left_buf.at[slot],
            load_sem.at[slot],
        )

    load_left(0, 0).start()
    load_right.wait()

    def turn(chunk):
        lanes = slice(chunk * CH, (chunk + 1) * CH)

        @pl.loop(0, d_block)
        def _(d):
            right_f32[pl.ds(d * vectors, vectors), :] = right_buf[d, :, lanes].astype(F32)

        @pl.loop(0, depth // CH)
        def _(k):
            vecs = CH // d_block
            rows = [
                right_f32[pl.ds(k * vecs + p, d_block, stride=vectors), :] for p in range(vecs)
            ]
            block = jnp.concatenate(rows, axis=0)
            at = pl.multiple_of(k * CH, CH)
            own[pl.ds(chunk * CH, CH), pl.ds(at, CH)] = block.T.astype(BF16)

    def remote(src, dst, send, recv, target):
        return pltpu.make_async_remote_copy(
            src_ref=src, dst_ref=dst, send_sem=send, recv_sem=recv, device_id=target,
            device_id_type=MESH,
        )

    def gather_copy(way, k):
        target = up if way == 0 else down
        at = way * CH
        if k < 3:
            chunk = k if way == 0 else 2 - k
            src = own.at[pl.ds(chunk * CH, CH), :]
            dst = got.at[k, pl.ds(at, CH), :]
        elif k == 3:
            src = got.at[0, pl.ds(at, CH), :]
            dst = got.at[3, pl.ds(at, CH), :]
        else:
            half = CH // 2
            src = got.at[1, pl.ds(at + way * half, half), :]
            dst = got.at[4, pl.ds(way * half, half), :]
        return remote(src, dst, ag_send.at[way, k], ag_recv.at[way, k], target)

    turn(0)
    pl.semaphore_wait(barrier, len(others))
    gather_copy(0, 0).start()
    turn(2)
    gather_copy(1, 0).start()
    turn(1)
    gather_copy(0, 1).start()
    gather_copy(1, 1).start()
    gather_copy(0, 2).start()
    gather_copy(1, 2).start()

    @pl.loop(0, vectors // PB)
    def _(block):
        slot = lax.rem(block, 2)
        load_left(block, slot).wait()

        @pl.when(block + 1 < vectors // PB)
        def _():
            load_left(block + 1, 1 - slot).start()

        @pl.loop(0, c_block // 8)
        def _(k):
            part = left_buf[slot, pl.ds(k * 8, 8)].astype(F32)
            for lane in range(width // 128):
                left_f32[lane, pl.ds(pl.multiple_of(k * 8 * PB, 8 * PB), 8 * PB), :] = part[
                    :, :, lane * 128 : (lane + 1) * 128
                ].reshape(8 * PB, 128)

        @pl.loop(0, PB // 2)
        def _(k):
            cols = [
                left_f32[lane, pl.ds(2 * k + q, c_block, stride=PB), :]
                for q in range(2)
                for lane in range(width // 128)
            ]
            vecs = jnp.concatenate(cols, axis=1).astype(BF16)
            half = jnp.dot(amp_ref[...], vecs, preferred_element_type=F32).astype(BF16)
            for q in range(2):
                at = pl.multiple_of((block * PB + 2 * k + q) * d_block, d_block)
                for ij in range(pairs):
                    halved[ij // 2, pl.ds(at, d_block), (ij % 2) * width : (ij % 2 + 1) * width] = (
                        half[ij * d_block : (ij + 1) * d_block, q * width : (q + 1) * width]
                    )

    rows_of = [CH * len(parts) for parts in GROUPS]
    start_of = [sum(rows_of[:g]) for g in range(NG)]

    def core_copy(g):
        lanes = pl.ds(pl.multiple_of((1 - c) * width, 128), width)
        return remote(
            prod.at[g % 2, :, pl.ds(0, rows_of[g]), lanes],
            core_got.at[:, pl.ds(start_of[g], rows_of[g]), :],
            core_send.at[g],
            core_recv.at[g],
            partner,
        )

    def multiply(g):
        rows = rows_of[g]
        if g < GATHERED:
            panel = own.at[pl.ds(start_of[g], rows), :]
        else:
            panel = got.at[g - GATHERED, pl.ds(0, rows), :]

        @pl.loop(0, (pairs // 2) * (2 * width // 256))
        def _(n):
            zz = n // (2 * width // 256)
            at = pl.multiple_of(lax.rem(n, 2 * width // 256) * 256, 256)
            prod[g % 2, zz, pl.ds(0, rows), pl.ds(at, 256)] = jnp.dot(
                panel[...], halved[zz, :, pl.ds(at, 256)], preferred_element_type=F32
            )

        core_copy(g).start()

    def z_copy(g, k):
        zz = lax.rem(z + k, 4)
        span = pl.ds(start_of[g], rows_of[g])
        return remote(
            chip.at[zz, span, :],
            z_got.at[k - 1, span, :],
            z_send.at[g, k - 1],
            z_recv.at[g, k - 1],
            device(y, x, zz, c),
        )

    def chip_sum(g):
        core_copy(g).wait()
        lanes = pl.ds(pl.multiple_of(c * width, 128), width)

        @pl.loop(0, (pairs // 2) * (rows_of[g] // 32))
        def _(n):
            zz = n // (rows_of[g] // 32)
            r = pl.multiple_of(lax.rem(n, rows_of[g] // 32) * 32, 32)
            total = prod[g % 2, zz, pl.ds(r, 32), lanes] + core_got[
                zz, pl.ds(start_of[g] + r, 32), :
            ]
            chip[zz, pl.ds(start_of[g] + r, 32), :] = total.astype(BF16)

        for k in (2, 1, 3):
            z_copy(g, k).start()

    def x_copy(g, i):
        offset, chunk = GROUPS[g][i]
        tile = lax.rem(y + offset, 4)
        span = pl.ds(start_of[g] + i * CH, CH)
        src = summed.at[span, :]
        dst = x_got.at[x, pl.ds(chunk * CH, CH), :]
        to_x, to_c = 2 * (tile // 2) + c, lax.rem(tile, 2)
        mine = jnp.logical_and(to_x == x, to_c == c)
        send, recv = x_send.at[g, i], x_recv.at[chunk, x]
        away = remote(src, dst, send, recv, device(y, to_x, z, to_c))
        here = pltpu.make_async_copy(src, dst, recv)
        return mine, away, here

    def z_sum(g):
        for k in (1, 2, 3):
            z_copy(g, k).wait_recv()

        @pl.loop(0, rows_of[g] // 32)
        def _(n):
            span = pl.ds(pl.multiple_of(start_of[g] + n * 32, 32), 32)
            total = chip[z, span, :].astype(F32)
            for k in range(3):
                total = total + z_got[k, span, :].astype(F32)
            summed[span, :] = total.astype(BF16)

        for i in range(len(GROUPS[g])):
            mine, away, here = x_copy(g, i)

            @pl.when(mine)
            def _():
                here.start()

            @pl.when(jnp.logical_not(mine))
            def _():
                away.start()

    own_tile = 2 * (x // 2) + c
    own_offset = lax.rem(own_tile - y + 4, 4)

    def x_sum(g):
        for offset, chunk in GROUPS[g]:

            @pl.when(own_offset == offset)
            def _():
                for k in range(4):
                    dst = x_got.at[k, pl.ds(chunk * CH, CH), :]
                    pltpu.make_async_copy(dst, dst, x_recv.at[chunk, k]).wait()

                @pl.loop(0, CH // 32)
                def _(n):
                    span = pl.ds(pl.multiple_of(chunk * CH + n * 32, 32), 32)
                    total = x_got[0, span, :].astype(F32)
                    for k in range(1, 4):
                        total = total + x_got[k, span, :].astype(F32)
                    out_ref[span, :] = total

    for g in range(NG):
        if g >= GATHERED:
            k = g - GATHERED
            for way in range(2):
                gather_copy(way, k).wait_recv()
            if k < 2:
                for way in range(2):
                    gather_copy(way, k + 3).start()
        multiply(g)
        chip_sum(g)
        if g >= 1:
            z_sum(g - 1)
        if g >= 2:
            x_sum(g - 2)
    z_sum(NG - 1)
    x_sum(NG - 2)
    x_sum(NG - 1)

    for way in range(2):
        for k in range(5):
            gather_copy(way, k).wait_send()
    for g in range(NG):
        for k in (1, 2, 3):
            z_copy(g, k).wait_send()
        for i in range(len(GROUPS[g])):
            mine, away, _ = x_copy(g, i)

            @pl.when(jnp.logical_not(mine))
            def _():
                away.wait_send()


def shards(left_vectors, right_vectors, amplitudes):
    pairs, d_block, c_block = amplitudes.shape
    _, vectors, width = left_vectors.shape
    depth = d_block * vectors
    rows = CH * sum(len(parts) for parts in GROUPS)
    big = 2 * CH
    dma = pltpu.SemaphoreType.DMA
    turned = pl.pallas_call(
        functools.partial(kernel, (pairs, d_block, c_block, vectors, width)),
        out_shape=jax.ShapeDtypeStruct((width, width), F32),
        in_specs=[
            pl.BlockSpec(memory_space=pltpu.VMEM),
            pl.BlockSpec(memory_space=pl.ANY),
            pl.BlockSpec(memory_space=pl.ANY),
        ],
        out_specs=pl.BlockSpec(memory_space=pltpu.VMEM),
        scratch_shapes=[
            pltpu.VMEM((2, c_block, PB, width), BF16),
            pltpu.VMEM((width // 128, c_block * PB, 128), F32),
            pltpu.VMEM((d_block, vectors, width), BF16),
            pltpu.VMEM((depth, CH), F32),
            pltpu.VMEM((width, depth), BF16),
            pltpu.VMEM((5, big, depth), BF16),
            pltpu.VMEM((pairs // 2, depth, 2 * width), BF16),
            pltpu.VMEM((2, pairs // 2, big, 2 * width), F32),
            pltpu.VMEM((pairs // 2, rows, width), F32),
            pltpu.VMEM((pairs // 2, rows, width), BF16),
            pltpu.VMEM((3, rows, width), BF16),
            pltpu.VMEM((rows, width), BF16),
            pltpu.VMEM((4, width, width), BF16),
            dma((2,)),
            dma,
            dma((2, 5)),
            dma((2, 5)),
            dma((NG,)),
            dma((NG,)),
            dma((NG, 3)),
            dma((NG, 3)),
            dma((NG, 2)),
            dma((3, 4)),
        ],
        compiler_params=pltpu.CompilerParams(
            collective_id=0, has_side_effects=True, vmem_limit_bytes=67_043_328
        ),
    )(amplitudes.reshape(pairs * d_block, c_block), left_vectors, right_vectors)
    return turned.T[None]


def solution(mesh):
    finer = Mesh(
        mesh.devices.reshape(mesh.shape["row"], 2, 2, 4, 2),
        ("row", "col_0", "col_1", "chol_0", "chol_1"),
    )
    placed = (P(None, COL_CHOL, "row"), P(None, COL_CHOL, "row"), P())
    return jax.shard_map(
        shards, mesh=finer, in_specs=placed, out_specs=P(CHOL, "row", COL), check_vma=False
    )
```

time: 330 us -> 117 us (0.35)
  the two profiles are of different devices: /device:TPU:1 before, /device:TPU:16 now
where the time goes in v1:
time: 117 us
  Pallas kernels  115 us (98%)
  local copies, waits for them, and re-layouts  2.11 us (2%)
    pallas_call x1, Pallas kernels, shards(): pl.pallas_call(functools.partial(kernel, (pairs, d_block, c_block, vector...  115 us

profile of v1, /device:TPU:16, one launch (start us, length us, event | category | flops | bytes accessed | tf_op | source)
XLA Modules:
  0.0 116.7 jit_solution(10274304041014501473)
XLA Ops:
  0.0 114.6 %shard_map.37 = f32[384,384]{1,0:T(8,128)} custom-call(bf16[128,64]{1,0:T(8,128)(2,1)} %bitcast.5, bf16[64,144,384]{2,1,0:T(8,128)(2,1)} %left_hbm.1, bf16[16,144,384]{2,1,0:T(8,128)(2,1)} %right_hbm.1), custom_call_target="tpu_custom_call" | custom-call | tf_op jit(solution)/shard_map/pallas_call | solution.py:315
  114.6 2.1 %copy.4 = f32[1,384,384]{2,1,0:T(8,128)} copy(f32[1,384,384]{1,2,0:T(8,128)} %bitcast.4) | data formatting | bytes 1179648 | tf_op jit(solution)/shard_map/broadcast_in_dim | solution.py:353

commit v2 on v1

v2 whole, which is shorter than its diff:
```python
import functools

import jax
import jax.numpy as jnp
from jax import lax
from jax.experimental import pallas as pl
from jax.experimental.pallas import tpu as pltpu
from jax.sharding import Mesh
from jax.sharding import PartitionSpec as P

COL = ("col_0", "col_1")
COL_CHOL = ("col_0", "col_1", "chol_0", "chol_1")
CHOL = ("chol_0", "chol_1")
MESH = pl.DeviceIdType.MESH
F32 = jnp.float32
BF16 = jnp.bfloat16
CH = 128
PB = 16

GROUPS = (
    ((0, 0, 256, "z"),),
    ((0, 256, 128, "z"),),
    ((3, 0, 128, "x"), (1, 256, 128, "x")),
    ((3, 128, 128, "z"), (1, 128, 128, "z")),
    ((2, 0, 128, "z"), (2, 256, 128, "x")),
    ((2, 128, 128, "z"),),
    ((3, 256, 64, "x"), (1, 0, 64, "x")),
    ((3, 320, 32, "z"), (3, 352, 32, "x"), (1, 64, 32, "z"), (1, 96, 32, "x")),
)
NG = len(GROUPS)
GATHERED = 2


class Part:
    def __init__(self, number, group, offset, tile_row, rows, first, row, row_z, row_x):
        self.number, self.group, self.offset, self.tile_row = number, group, offset, tile_row
        self.rows, self.first, self.row, self.row_z, self.row_x = rows, first, row, row_z, row_x


def laid_out():
    parts, row, row_z, row_x = [], 0, 0, 0
    for g, group in enumerate(GROUPS):
        shared = 0
        for offset, tile_row, rows, first in group:
            parts.append(Part(len(parts), g, offset, tile_row, rows, first, row, row_z, row_x))
            row += rows
            if first == "z":
                row_z += rows
            else:
                shared = rows
        row_x += shared
    return parts, row, row_z, row_x


PARTS, ROWS, ROWS_Z, ROWS_X = laid_out()


def where():
    return dict(
        y=lax.axis_index("row"),
        x=lax.axis_index("col_0") * 2 + lax.axis_index("chol_1"),
        z=lax.axis_index("chol_0"),
        c=lax.axis_index("col_1"),
    )


def device(y, x, z, c):
    return (y, x // 2, c, z, lax.rem(x, 2))


def kernel(
    sizes, amp_ref, left_hbm, right_hbm, out_ref,
    left_buf, left_f32, right_buf, right_f32, own, got, halved, prod, core_got, chip, z_got,
    z_total, x_got, x_total, last_got,
    load_sem, right_sem, ag_send, ag_recv, core_send, core_recv, z_send, z_recv, x_send, x_recv,
    last_send, last_recv,
):
    pairs, d_block, c_block, vectors, width = sizes
    depth = d_block * vectors
    me = where()
    y, x, z, c = me["y"], me["x"], me["z"], me["c"]
    up = device(lax.rem(y + 1, 4), x, z, c)
    down = device(lax.rem(y + 3, 4), x, z, c)
    partner = device(y, x, z, 1 - c)

    barrier = pltpu.get_barrier_semaphore()
    others = [up, down, partner]
    others += [device(y, x, lax.rem(z + k, 4), q) for k in (1, 2, 3) for q in (c, 1 - c)]
    others += [device(y, lax.rem(x + k, 4), z, q) for k in (1, 2, 3) for q in (c, 1 - c)]
    for other in others:
        pl.semaphore_signal(barrier, inc=1, device_id=other, device_id_type=MESH)

    def load_right(chunk):
        lanes = pl.ds(chunk * CH, CH)
        return pltpu.make_async_copy(
            right_hbm.at[:, :, lanes], right_buf.at[chunk], right_sem.at[chunk]
        )

    for chunk in (0, 2, 1):
        load_right(chunk).start()

    def load_left(block, slot):
        return pltpu.make_async_copy(
            left_hbm.at[:, pl.ds(pl.multiple_of(block * PB, PB), PB), :],
            left_buf.at[slot],
            load_sem.at[slot],
        )

    load_left(0, 0).start()

    def turn(chunk):
        load_right(chunk).wait()

        @pl.loop(0, d_block, unroll=4)
        def _(d):
            right_f32[pl.ds(d * vectors, vectors), :] = right_buf[chunk, d].astype(F32)

        @pl.loop(0, depth // CH, unroll=6)
        def _(k):
            vecs = CH // d_block
            rows = [
                right_f32[pl.ds(k * vecs + p, d_block, stride=vectors), :] for p in range(vecs)
            ]
            block = jnp.concatenate(rows, axis=0).astype(BF16)
            own[pl.ds(chunk * CH, CH), pl.ds(pl.multiple_of(k * CH, CH), CH)] = block.T

    def remote(src, dst, send, recv, target):
        return pltpu.make_async_remote_copy(
            src_ref=src, dst_ref=dst, send_sem=send, recv_sem=recv, device_id=target,
            device_id_type=MESH,
        )

    rows_of = [sum(p.rows for p in PARTS if p.group == g) for g in range(NG)]
    start_of = [sum(rows_of[:g]) for g in range(NG)]

    def gather_copy(way, k):
        target = up if way == 0 else down
        first = start_of[GATHERED]
        half = rows_of[GATHERED + k] // 2
        dst = got.at[pl.ds(start_of[GATHERED + k] - first + way * half, half), :]
        if k in (2, 3):
            at = start_of[GATHERED + k - 2] - first + way * CH + (way * half if k == 3 else 0)
            src = got.at[pl.ds(at, half), :]
        else:
            chunk = min(k, 2) if way == 0 else 2 - min(k, 2)
            src = own.at[pl.ds(chunk * CH + (half if k == 5 else 0), half), :]
        return remote(src, dst, ag_send.at[way, k], ag_recv.at[way, k], target)

    turn(0)
    pl.semaphore_wait(barrier, len(others))
    gather_copy(0, 0).start()
    turn(2)
    gather_copy(1, 0).start()
    turn(1)
    gather_copy(0, 1).start()
    gather_copy(1, 1).start()

    @pl.loop(0, vectors // PB)
    def _(block):
        slot = lax.rem(block, 2)
        load_left(block, slot).wait()

        @pl.when(block + 1 < vectors // PB)
        def _():
            load_left(block + 1, 1 - slot).start()

        @pl.loop(0, c_block // 8, unroll=4)
        def _(k):
            part = left_buf[slot, pl.ds(k * 8, 8)].astype(F32)
            for lane in range(width // 128):
                left_f32[lane, pl.ds(pl.multiple_of(k * 8 * PB, 8 * PB), 8 * PB), :] = part[
                    :, :, lane * 128 : (lane + 1) * 128
                ].reshape(8 * PB, 128)

        @pl.loop(0, PB // 2, unroll=8)
        def _(k):
            cols = [
                left_f32[lane, pl.ds(2 * k + q, c_block, stride=PB), :]
                for q in range(2)
                for lane in range(width // 128)
            ]
            vecs = jnp.concatenate(cols, axis=1).astype(BF16)
            half = jnp.dot(amp_ref[...], vecs, preferred_element_type=F32).astype(BF16)
            for q in range(2):
                at = pl.multiple_of((block * PB + 2 * k + q) * d_block, d_block)
                for ij in range(pairs):
                    halved[ij // 2, pl.ds(at, d_block), (ij % 2) * width : (ij % 2 + 1) * width] = (
                        half[ij * d_block : (ij + 1) * d_block, q * width : (q + 1) * width]
                    )

    halves = pairs // 2
    step = 64

    def core_copy(g, zz):
        lanes = pl.ds(pl.multiple_of((1 - c) * width, 128), width)
        return remote(
            prod.at[g % 2, zz, pl.ds(0, rows_of[g]), lanes],
            core_got.at[zz, pl.ds(start_of[g], rows_of[g]), :],
            core_send.at[g, zz],
            core_recv.at[g, zz],
            partner,
        )

    def multiply(g):
        rows = rows_of[g]
        if g < GATHERED:
            panel = own.at[pl.ds(start_of[g], rows), :]
        else:
            panel = got.at[pl.ds(start_of[g] - start_of[GATHERED], rows), :]

        @pl.loop(0, halves, unroll=2 if rows > CH else 4)
        def _(i):
            zz = lax.rem(z + 1 + i, 4)
            prod[g % 2, zz, pl.ds(0, rows), :] = jnp.dot(
                panel[...], halved[zz], preferred_element_type=F32
            )
            core_copy(g, zz).start()

    def place(part):
        tile = lax.rem(y + part.offset, 4)
        return tile // 2, lax.rem(tile, 2)

    def z_copy(part, k):
        zz = lax.rem(z + k, 4)
        return remote(
            chip.at[zz, pl.ds(part.row, part.rows), :],
            z_got.at[k - 1, pl.ds(part.row_z, part.rows), :],
            z_send.at[part.number, k - 1],
            z_recv.at[part.number, k - 1],
            device(y, x, zz, c),
        )

    def x_copy(part, zz):
        to_x = 2 * place(part)[0] + c
        slot = lax.rem(x - to_x + 7, 4)
        return to_x != x, remote(
            chip.at[zz, pl.ds(part.row, part.rows), :],
            x_got.at[slot, zz, pl.ds(part.row_x, part.rows), :],
            x_send.at[part.number, zz],
            x_recv.at[part.group, slot, zz],
            device(y, to_x, z, c),
        )

    def sums_over_x(part):
        return 2 * place(part)[0] + c == x

    def chip_sum(g):
        lanes = pl.ds(pl.multiple_of(c * width, 128), width)
        for i in range(halves):
            zz = lax.rem(z + 1 + i, 4)
            core_copy(g, zz).wait()

            @pl.loop(0, rows_of[g] // step)
            def _(n):
                r = pl.multiple_of(n * step, step)
                at = pl.ds(pl.multiple_of(start_of[g] + r, step), step)
                total = prod[g % 2, zz, pl.ds(r, step), lanes] + core_got[zz, at, :]
                chip[zz, at, :] = total.astype(BF16)

            for part in PARTS:
                if part.group != g:
                    continue
                if part.first == "z":
                    if i < halves - 1:
                        z_copy(part, i + 1).start()
                else:
                    away, copy = x_copy(part, zz)

                    @pl.when(away)
                    def _():
                        copy.start()

    def last_copies(part):
        to_c = place(part)[1]
        if part.first == "z":
            to_x = 2 * place(part)[0] + c
            ends = [(z_total.at[pl.ds(part.row_z, part.rows), :], x, to_x, z)]
        else:
            ends = [
                (x_total.at[zz, pl.ds(part.row_x, part.rows), :], z, x, zz) for zz in range(halves)
            ]
        copies = []
        for k, (src, slot, to_x, to_z) in enumerate(ends):
            dst = last_got.at[slot, pl.ds(part.tile_row, part.rows), :]
            recv = last_recv.at[part.number, slot]
            mine = jnp.logical_and(jnp.logical_and(to_x == x, to_z == z), to_c == c)
            away = remote(
                src, dst, last_send.at[part.number, k], recv, device(y, to_x, to_z, to_c)
            )
            copies.append((mine, away, pltpu.make_async_copy(src, dst, recv)))
        return copies

    def send_last(part):
        for mine, away, here in last_copies(part):

            @pl.when(mine)
            def _():
                here.start()

            @pl.when(jnp.logical_not(mine))
            def _():
                away.start()

    def wait_last(part):
        for mine, away, _ in last_copies(part):

            @pl.when(jnp.logical_not(mine))
            def _():
                away.wait_send()

    def second(g):
        for part in PARTS:
            if part.group != g:
                continue
            if part.first == "z":
                for k in (1, 2, 3):
                    z_copy(part, k).wait_recv()

                step = min(part.rows, 64)

                @pl.loop(0, part.rows // step)
                def _(n):
                    total = chip[z, pl.ds(part.row + n * step, step), :].astype(F32)
                    at = pl.ds(part.row_z + n * step, step)
                    for k in range(3):
                        total = total + z_got[k, at, :].astype(F32)
                    z_total[at, :] = total.astype(BF16)

                send_last(part)
            else:

                @pl.when(sums_over_x(part))
                def _():
                    at = pl.ds(part.row_x, part.rows)
                    step = min(part.rows, 64)
                    for k in range(3):
                        for zz in range(halves):
                            dst = x_got.at[k, zz, at, :]
                            pltpu.make_async_copy(dst, dst, x_recv.at[g, k, zz]).wait()

                    @pl.loop(0, halves * (part.rows // step))
                    def _(n):
                        zz, r = n // (part.rows // step), lax.rem(n, part.rows // step) * step
                        r = pl.multiple_of(r, step)
                        total = chip[zz, pl.ds(part.row + r, step), :].astype(F32)
                        at = pl.ds(part.row_x + r, step)
                        for k in range(3):
                            total = total + x_got[k, zz, at, :].astype(F32)
                        x_total[zz, at, :] = total.astype(BF16)

                    send_last(part)

    own_tile = 2 * (x // 2) + c
    own_offset = lax.rem(own_tile - y + 4, 4)

    def final(g):
        for part in PARTS:
            if part.group != g:
                continue

            @pl.when(own_offset == part.offset)
            def _():
                for k in range(4):
                    dst = last_got.at[k, pl.ds(part.tile_row, part.rows), :]
                    pltpu.make_async_copy(dst, dst, last_recv.at[part.number, k]).wait()

                step = min(part.rows, 64)

                @pl.loop(0, part.rows // step)
                def _(n):
                    at = pl.ds(part.tile_row + n * step, step)
                    total = last_got[0, at, :].astype(F32)
                    for k in range(1, 4):
                        total = total + last_got[k, at, :].astype(F32)
                    out_ref[at, :] = total

    for g in range(NG):
        if g >= GATHERED:
            k = g - GATHERED
            for way in range(2):
                gather_copy(way, k).wait_recv()
            if k < 2:
                for step_on in ((2,), (3, 4, 5))[k]:
                    for way in range(2):
                        gather_copy(way, step_on).start()
        multiply(g)
        chip_sum(g)
        if g >= 1:
            second(g - 1)
        if g >= 2:
            final(g - 2)
    second(NG - 1)
    final(NG - 2)
    final(NG - 1)

    for way in range(2):
        for k in range(6):
            gather_copy(way, k).wait_send()
    for part in PARTS:
        if part.first == "z":
            for k in (1, 2, 3):
                z_copy(part, k).wait_send()
            wait_last(part)
        else:
            for zz in range(halves):
                away, copy = x_copy(part, zz)

                @pl.when(away)
                def _():
                    copy.wait_send()

            @pl.when(sums_over_x(part))
            def _():
                wait_last(part)


def shards(left_vectors, right_vectors, amplitudes):
    pairs, d_block, c_block = amplitudes.shape
    _, vectors, width = left_vectors.shape
    depth = d_block * vectors
    big = 2 * CH
    dma = pltpu.SemaphoreType.DMA
    turned = pl.pallas_call(
        functools.partial(kernel, (pairs, d_block, c_block, vectors, width)),
        out_shape=jax.ShapeDtypeStruct((width, width), F32),
        in_specs=[
            pl.BlockSpec(memory_space=pltpu.VMEM),
            pl.BlockSpec(memory_space=pl.ANY),
            pl.BlockSpec(memory_space=pl.ANY),
        ],
        out_specs=pl.BlockSpec(memory_space=pltpu.VMEM),
        scratch_shapes=[
            pltpu.VMEM((2, c_block, PB, width), BF16),
            pltpu.VMEM((width // 128, c_block * PB, 128), F32),
            pltpu.VMEM((width // CH, d_block, vectors, CH), BF16),
            pltpu.VMEM((depth, CH), F32),
            pltpu.VMEM((width, depth), BF16),
            pltpu.VMEM((ROWS - width, depth), BF16),
            pltpu.VMEM((pairs // 2, depth, 2 * width), BF16),
            pltpu.VMEM((2, pairs // 2, big, 2 * width), F32),
            pltpu.VMEM((pairs // 2, ROWS, width), F32),
            pltpu.VMEM((pairs // 2, ROWS, width), BF16),
            pltpu.VMEM((3, ROWS_Z, width), BF16),
            pltpu.VMEM((ROWS_Z, width), BF16),
            pltpu.VMEM((3, pairs // 2, ROWS_X, width), BF16),
            pltpu.VMEM((pairs // 2, ROWS_X, width), BF16),
            pltpu.VMEM((4, width, width), BF16),
            dma((2,)),
            dma((width // CH,)),
            dma((2, 6)),
            dma((2, 6)),
            dma((NG, pairs // 2)),
            dma((NG, pairs // 2)),
            dma((len(PARTS), 3)),
            dma((len(PARTS), 3)),
            dma((len(PARTS), pairs // 2)),
            dma((NG, 3, pairs // 2)),
            dma((len(PARTS), 4)),
            dma((len(PARTS), 4)),
        ],
        compiler_params=pltpu.CompilerParams(
            collective_id=0, has_side_effects=True, vmem_limit_bytes=67_043_328
        ),
    )(amplitudes.reshape(pairs * d_block, c_block), left_vectors, right_vectors)
    return turned.T[None]


def solution(mesh):
    finer = Mesh(
        mesh.devices.reshape(mesh.shape["row"], 2, 2, 4, 2),
        ("row", "col_0", "col_1", "chol_0", "chol_1"),
    )
    placed = (P(None, COL_CHOL, "row"), P(None, COL_CHOL, "row"), P())
    return jax.shard_map(
        shards, mesh=finer, in_specs=placed, out_specs=P(CHOL, "row", COL), check_vma=False
    )
```

time: 117 us -> 97.3 us (0.83)
  the two profiles are of different devices: /device:TPU:16 before, /device:TPU:1 now
where the time goes in v2:
time: 97.3 us; the launch traced here: 96.7 us
  Pallas kernels  94.6 us (97%)
  local copies, waits for them, and re-layouts  2.11 us (2%)
    pallas_call x1, Pallas kernels, shards(): pl.pallas_call(functools.partial(kernel, (pairs, d_block, c_block, vector...  94.6 us
    broadcast_in_dim x1, local copies, waits for them, and re-layouts, shards(): return turned.T[None]  2.11 us

profile of v2, /device:TPU:1, one launch (start us, length us, event | category | flops | bytes accessed | tf_op | source)
XLA Modules:
  0.0 96.7 jit_solution(12036392381485634131)
XLA Ops:
  0.0 94.6 %shard_map.37 = f32[384,384]{1,0:T(8,128)} custom-call(bf16[128,64]{1,0:T(8,128)(2,1)} %bitcast.5, bf16[64,144,384]{2,1,0:T(8,128)(2,1)} %left_hbm.1, bf16[16,144,384]{2,1,0:T(8,128)(2,1)} %right_hbm.1), custom_call_target="tpu_custom_call" | custom-call | tf_op jit(solution)/shard_map/pallas_call | solution.py:423
  94.6 2.1 %copy.4 = f32[1,384,384]{2,1,0:T(8,128)} copy(f32[1,384,384]{1,2,0:T(8,128)} %bitcast.4) | data formatting | bytes 1179648 | tf_op jit(solution)/shard_map/broadcast_in_dim | solution.py:465

commit v3 on v2

--- a/solution.py
+++ b/solution.py
@@ -22,13 +22,24 @@
     ((0, 256, 128, "z"),),
     ((3, 0, 128, "x"), (1, 256, 128, "x")),
     ((3, 128, 128, "z"), (1, 128, 128, "z")),
-    ((2, 0, 128, "z"), (2, 256, 128, "x")),
+    ((2, 0, 128, "z"), (2, 256, 128, "z")),
     ((2, 128, 128, "z"),),
     ((3, 256, 64, "x"), (1, 0, 64, "x")),
-    ((3, 320, 32, "z"), (3, 352, 32, "x"), (1, 64, 32, "z"), (1, 96, 32, "x")),
+    ((3, 320, 64, "z"), (1, 64, 64, "z")),
 )
 NG = len(GROUPS)
 GATHERED = 2
+ORDER = (
+    ("mul", 0), ("mul", 1), ("chip", 0), ("chip", 1),
+    ("get", 2), ("mul", 2), ("chip", 2),
+    ("get", 3), ("mul", 3), ("second", 0), ("chip", 3), ("second", 1), ("second", 2),
+    ("final", 0), ("final", 1),
+    ("get", 4), ("mul", 4), ("chip", 4), ("second", 3), ("final", 2),
+    ("get", 5), ("mul", 5), ("chip", 5),
+    ("get", 6), ("mul", 6), ("chip", 6), ("second", 4),
+    ("get", 7), ("mul", 7), ("chip", 7), ("second", 5), ("final", 3), ("second", 6), ("final", 4),
+    ("second", 7), ("final", 5), ("final", 6), ("final", 7),
+)
 
 
 class Part:
@@ -133,6 +144,9 @@
     rows_of = [sum(p.rows for p in PARTS if p.group == g) for g in range(NG)]
     start_of = [sum(rows_of[:g]) for g in range(NG)]
 
+    def landed(ref, sem):
+        pltpu.make_async_copy(ref, ref, sem).wait()
+
     def gather_copy(way, k):
         target = up if way == 0 else down
         first = start_of[GATHERED]
@@ -143,8 +157,9 @@
             src = got.at[pl.ds(at, half), :]
         else:
             chunk = min(k, 2) if way == 0 else 2 - min(k, 2)
-            src = own.at[pl.ds(chunk * CH + (half if k == 5 else 0), half), :]
-        return remote(src, dst, ag_send.at[way, k], ag_recv.at[way, k], target)
+            past = sum(rows_of[GATHERED + 4 : GATHERED + k]) // 2
+            src = own.at[pl.ds(chunk * CH + past, half), :]
+        return remote(src, dst, ag_send.at[way], ag_recv.at[k], target)
 
     turn(0)
     pl.semaphore_wait(barrier, len(others))
@@ -191,13 +206,13 @@
     halves = pairs // 2
     step = 64
 
-    def core_copy(g, zz):
+    def core_copy(g, pair, zz):
         lanes = pl.ds(pl.multiple_of((1 - c) * width, 128), width)
         return remote(
             prod.at[g % 2, zz, pl.ds(0, rows_of[g]), lanes],
             core_got.at[zz, pl.ds(start_of[g], rows_of[g]), :],
-            core_send.at[g, zz],
-            core_recv.at[g, zz],
+            core_send.at[g % 2, pair],
+            core_recv.at[g, pair],
             partner,
         )
 
@@ -208,13 +223,15 @@
         else:
             panel = got.at[pl.ds(start_of[g] - start_of[GATHERED], rows), :]
 
-        @pl.loop(0, halves, unroll=2 if rows > CH else 4)
+        @pl.loop(0, halves // 2)
         def _(i):
-            zz = lax.rem(z + 1 + i, 4)
-            prod[g % 2, zz, pl.ds(0, rows), :] = jnp.dot(
-                panel[...], halved[zz], preferred_element_type=F32
-            )
-            core_copy(g, zz).start()
+            two = [lax.rem(z + 1 + 2 * i + q, 4) for q in range(2)]
+            for zz in two:
+                prod[g % 2, zz, pl.ds(0, rows), :] = jnp.dot(
+                    panel[...], halved[zz], preferred_element_type=F32
+                )
+            for zz in two:
+                core_copy(g, i, zz).start()
 
     def place(part):
         tile = lax.rem(y + part.offset, 4)
@@ -225,8 +242,8 @@
         return remote(
             chip.at[zz, pl.ds(part.row, part.rows), :],
             z_got.at[k - 1, pl.ds(part.row_z, part.rows), :],
-            z_send.at[part.number, k - 1],
-            z_recv.at[part.number, k - 1],
+            z_send,
+            z_recv.at[part.number],
             device(y, x, zz, c),
         )
 
@@ -236,8 +253,8 @@
         return to_x != x, remote(
             chip.at[zz, pl.ds(part.row, part.rows), :],
             x_got.at[slot, zz, pl.ds(part.row_x, part.rows), :],
-            x_send.at[part.number, zz],
-            x_recv.at[part.group, slot, zz],
+            x_send.at[part.number],
+            x_recv.at[part.group],
             device(y, to_x, z, c),
         )
 
@@ -248,7 +265,10 @@
         lanes = pl.ds(pl.multiple_of(c * width, 128), width)
         for i in range(halves):
             zz = lax.rem(z + 1 + i, 4)
-            core_copy(g, zz).wait()
+            if i % 2 == 0:
+                both = core_got.at[pl.ds(0, 2), pl.ds(start_of[g], rows_of[g]), :]
+                landed(both, core_recv.at[g, i // 2])
+                landed(both, core_send.at[g % 2, i // 2])
 
             @pl.loop(0, rows_of[g] // step)
             def _(n):
@@ -280,12 +300,12 @@
                 (x_total.at[zz, pl.ds(part.row_x, part.rows), :], z, x, zz) for zz in range(halves)
             ]
         copies = []
-        for k, (src, slot, to_x, to_z) in enumerate(ends):
+        for src, slot, to_x, to_z in ends:
             dst = last_got.at[slot, pl.ds(part.tile_row, part.rows), :]
-            recv = last_recv.at[part.number, slot]
+            recv = last_recv.at[part.number]
             mine = jnp.logical_and(jnp.logical_and(to_x == x, to_z == z), to_c == c)
             away = remote(
-                src, dst, last_send.at[part.number, k], recv, device(y, to_x, to_z, to_c)
+                src, dst, last_send.at[part.number], recv, device(y, to_x, to_z, to_c)
             )
             copies.append((mine, away, pltpu.make_async_copy(src, dst, recv)))
         return copies
@@ -302,19 +322,31 @@
                 away.start()
 
     def wait_last(part):
-        for mine, away, _ in last_copies(part):
+        if part.first == "z":
+            ((mine, away, _),) = last_copies(part)
 
             @pl.when(jnp.logical_not(mine))
             def _():
                 away.wait_send()
+
+        else:
+            at = pl.ds(part.row_x, part.rows)
+            stays = place(part)[1] == c
+
+            @pl.when(stays)
+            def _():
+                landed(x_total.at[pl.ds(0, halves - 1), at, :], last_send.at[part.number])
+
+            @pl.when(jnp.logical_not(stays))
+            def _():
+                landed(x_total.at[:, at, :], last_send.at[part.number])
 
     def second(g):
         for part in PARTS:
             if part.group != g:
                 continue
             if part.first == "z":
-                for k in (1, 2, 3):
-                    z_copy(part, k).wait_recv()
+                landed(z_got.at[:, pl.ds(part.row_z, part.rows), :], z_recv.at[part.number])
 
                 step = min(part.rows, 64)
 
@@ -333,10 +365,7 @@
                 def _():
                     at = pl.ds(part.row_x, part.rows)
                     step = min(part.rows, 64)
-                    for k in range(3):
-                        for zz in range(halves):
-                            dst = x_got.at[k, zz, at, :]
-                            pltpu.make_async_copy(dst, dst, x_recv.at[g, k, zz]).wait()
+                    landed(x_got.at[:, :, at, :], x_recv.at[g])
 
                     @pl.loop(0, halves * (part.rows // step))
                     def _(n):
@@ -360,9 +389,8 @@
 
             @pl.when(own_offset == part.offset)
             def _():
-                for k in range(4):
-                    dst = last_got.at[k, pl.ds(part.tile_row, part.rows), :]
-                    pltpu.make_async_copy(dst, dst, last_recv.at[part.number, k]).wait()
+                arrived = last_got.at[:, pl.ds(part.tile_row, part.rows), :]
+                landed(arrived, last_recv.at[part.number])
 
                 step = min(part.rows, 64)
 
@@ -374,40 +402,30 @@
                         total = total + last_got[k, at, :].astype(F32)
                     out_ref[at, :] = total
 
-    for g in range(NG):
-        if g >= GATHERED:
-            k = g - GATHERED
+    def gathered(g):
+        k = g - GATHERED
+        span = pl.ds(start_of[g] - start_of[GATHERED], rows_of[g])
+        landed(got.at[span, :], ag_recv.at[k])
+        for step_on in {0: (2,), 1: range(3, NG - GATHERED)}.get(k, ()):
             for way in range(2):
-                gather_copy(way, k).wait_recv()
-            if k < 2:
-                for step_on in ((2,), (3, 4, 5))[k]:
-                    for way in range(2):
-                        gather_copy(way, step_on).start()
-        multiply(g)
-        chip_sum(g)
-        if g >= 1:
-            second(g - 1)
-        if g >= 2:
-            final(g - 2)
-    second(NG - 1)
-    final(NG - 2)
-    final(NG - 1)
+                gather_copy(way, step_on).start()
+
+    steps = dict(get=gathered, mul=multiply, chip=chip_sum, second=second, final=final)
+    for name, g in ORDER:
+        steps[name](g)
 
     for way in range(2):
-        for k in range(6):
-            gather_copy(way, k).wait_send()
+        landed(got.at[pl.ds(0, (ROWS - width) // 2), :], ag_send.at[way])
+    landed(z_got, z_send)
     for part in PARTS:
         if part.first == "z":
-            for k in (1, 2, 3):
-                z_copy(part, k).wait_send()
             wait_last(part)
         else:
-            for zz in range(halves):
-                away, copy = x_copy(part, zz)
-
-                @pl.when(away)
-                def _():
-                    copy.wait_send()
+            away, _ = x_copy(part, 0)
+
+            @pl.when(away)
+            def _():
+                landed(chip.at[:, pl.ds(part.row, part.rows), :], x_send.at[part.number])
 
             @pl.when(sums_over_x(part))
             def _():
@@ -447,16 +465,16 @@
             pltpu.VMEM((4, width, width), BF16),
             dma((2,)),
             dma((width // CH,)),
-            dma((2, 6)),
-            dma((2, 6)),
-            dma((NG, pairs // 2)),
-            dma((NG, pairs // 2)),
-            dma((len(PARTS), 3)),
-            dma((len(PARTS), 3)),
-            dma((len(PARTS), pairs // 2)),
-            dma((NG, 3, pairs // 2)),
-            dma((len(PARTS), 4)),
-            dma((len(PARTS), 4)),
+            dma((2,)),
+            dma((NG - GATHERED,)),
+            dma((2, 2)),
+            dma((NG, 2)),
+            dma,
+            dma((len(PARTS),)),
+            dma((len(PARTS),)),
+            dma((NG,)),
+            dma((len(PARTS),)),
+            dma((len(PARTS),)),
         ],
         compiler_params=pltpu.CompilerParams(
             collective_id=0, has_side_effects=True, vmem_limit_bytes=67_043_328

time: 97.3 us -> 86 us (0.88)
  Pallas kernels: 94.6 us -> 83.3 us
    pallas_call x1, Pallas kernels: 94.6 us -> 83.3 us  [shards(): pl.pallas_call(functools.partial(kernel, (pairs, d_block, c_block, vector...]
where the time goes in v3:
time: 86 us; the launch traced here: 85.4 us
  Pallas kernels  83.3 us (97%)
  local copies, waits for them, and re-layouts  2.11 us (2%)
    pallas_call x1, Pallas kernels, shards(): pl.pallas_call(functools.partial(kernel, (pairs, d_block, c_block, vector...  83.3 us
    broadcast_in_dim x1, local copies, waits for them, and re-layouts, shards(): return turned.T[None]  2.11 us

profile of v3, /device:TPU:1, one launch (start us, length us, event | category | flops | bytes accessed | tf_op | source)
XLA Modules:
  0.0 85.4 jit_solution(1334347693699322197)
XLA Ops:
  0.0 83.3 %shard_map.37 = f32[384,384]{1,0:T(8,128)} custom-call(bf16[128,64]{1,0:T(8,128)(2,1)} %bitcast.5, bf16[64,144,384]{2,1,0:T(8,128)(2,1)} %left_hbm.1, bf16[16,144,384]{2,1,0:T(8,128)(2,1)} %right_hbm.1), custom_call_target="tpu_custom_call" | custom-call | tf_op jit(solution)/shard_map/pallas_call | solution.py:441
  83.3 2.1 %copy.4 = f32[1,384,384]{2,1,0:T(8,128)} copy(f32[1,384,384]{1,2,0:T(8,128)} %bitcast.4) | data formatting | bytes 1179648 | tf_op jit(solution)/shard_map/broadcast_in_dim | solution.py:483

commit v4 on v3

--- a/solution.py
+++ b/solution.py
@@ -24,8 +24,8 @@
     ((3, 128, 128, "z"), (1, 128, 128, "z")),
     ((2, 0, 128, "z"), (2, 256, 128, "z")),
     ((2, 128, 128, "z"),),
-    ((3, 256, 64, "x"), (1, 0, 64, "x")),
-    ((3, 320, 64, "z"), (1, 64, 64, "z")),
+    ((3, 256, 64, "z"), (1, 0, 64, "z")),
+    ((3, 320, 32, "z"), (3, 352, 32, "x"), (1, 64, 32, "z"), (1, 96, 32, "x")),
 )
 NG = len(GROUPS)
 GATHERED = 2
@@ -33,12 +33,11 @@
     ("mul", 0), ("mul", 1), ("chip", 0), ("chip", 1),
     ("get", 2), ("mul", 2), ("chip", 2),
     ("get", 3), ("mul", 3), ("second", 0), ("chip", 3), ("second", 1), ("second", 2),
-    ("final", 0), ("final", 1),
-    ("get", 4), ("mul", 4), ("chip", 4), ("second", 3), ("final", 2),
-    ("get", 5), ("mul", 5), ("chip", 5),
+    ("get", 4), ("mul", 4), ("chip", 4), ("second", 3), ("final", 0), ("final", 1),
+    ("get", 5), ("mul", 5), ("chip", 5), ("final", 2),
     ("get", 6), ("mul", 6), ("chip", 6), ("second", 4),
-    ("get", 7), ("mul", 7), ("chip", 7), ("second", 5), ("final", 3), ("second", 6), ("final", 4),
-    ("second", 7), ("final", 5), ("final", 6), ("final", 7),
+    ("get", 7), ("mul", 7), ("chip", 7), ("second", 5), ("second", 6), ("second", 7),
+    ("final", 3), ("final", 4), ("final", 5), ("final", 6), ("final", 7),
 )
 
 
@@ -225,7 +224,7 @@
 
         @pl.loop(0, halves // 2)
         def _(i):
-            two = [lax.rem(z + 1 + 2 * i + q, 4) for q in range(2)]
+            two = [lax.rem(z + 2 + i, 4), lax.rem(z + 1 + 3 * i, 4)]
             for zz in two:
                 prod[g % 2, zz, pl.ds(0, rows), :] = jnp.dot(
                     panel[...], halved[zz], preferred_element_type=F32
@@ -263,8 +262,8 @@
 
     def chip_sum(g):
         lanes = pl.ds(pl.multiple_of(c * width, 128), width)
-        for i in range(halves):
-            zz = lax.rem(z + 1 + i, 4)
+        for i, ahead in enumerate((2, 1, 3, 0)):
+            zz = lax.rem(z + ahead, 4)
             if i % 2 == 0:
                 both = core_got.at[pl.ds(0, 2), pl.ds(start_of[g], rows_of[g]), :]
                 landed(both, core_recv.at[g, i // 2])
@@ -281,8 +280,8 @@
                 if part.group != g:
                     continue
                 if part.first == "z":
-                    if i < halves - 1:
-                        z_copy(part, i + 1).start()
+                    if ahead:
+                        z_copy(part, ahead).start()
                 else:
                     away, copy = x_copy(part, zz)
 

time: 86 us -> 84.2 us (0.979)
  Pallas kernels: 83.3 us -> 81.5 us
    pallas_call x1, Pallas kernels: 83.3 us -> 81.5 us  [shards(): pl.pallas_call(functools.partial(kernel, (pairs, d_block, c_block, vector...]
where the time goes in v4:
time: 84.2 us; the launch traced here: 83.6 us
  Pallas kernels  81.5 us (97%)
  local copies, waits for them, and re-layouts  2.11 us (3%)
    pallas_call x1, Pallas kernels, shards(): pl.pallas_call(functools.partial(kernel, (pairs, d_block, c_block, vector...  81.5 us
    broadcast_in_dim x1, local copies, waits for them, and re-layouts, shards(): return turned.T[None]  2.11 us

profile of v4, /device:TPU:1, one launch (start us, length us, event | category | flops | bytes accessed | tf_op | source)
XLA Modules:
  0.0 83.6 jit_solution(5083869693852327125)
XLA Ops:
  0.0 81.5 %shard_map.37 = f32[384,384]{1,0:T(8,128)} custom-call(bf16[128,64]{1,0:T(8,128)(2,1)} %bitcast.5, bf16[64,144,384]{2,1,0:T(8,128)(2,1)} %left_hbm.1, bf16[16,144,384]{2,1,0:T(8,128)(2,1)} %right_hbm.1), custom_call_target="tpu_custom_call" | custom-call | tf_op jit(solution)/shard_map/pallas_call | solution.py:440
  81.5 2.1 %copy.4 = f32[1,384,384]{2,1,0:T(8,128)} copy(f32[1,384,384]{1,2,0:T(8,128)} %bitcast.4) | data formatting | bytes 1179648 | tf_op jit(solution)/shard_map/broadcast_in_dim | solution.py:482

commit v5 on v4

--- a/solution.py
+++ b/solution.py
@@ -23,7 +23,7 @@
     ((3, 0, 128, "x"), (1, 256, 128, "x")),
     ((3, 128, 128, "z"), (1, 128, 128, "z")),
     ((2, 0, 128, "z"), (2, 256, 128, "z")),
-    ((2, 128, 128, "z"),),
+    ((2, 128, 64, "z"), (2, 192, 64, "x")),
     ((3, 256, 64, "z"), (1, 0, 64, "z")),
     ((3, 320, 32, "z"), (3, 352, 32, "x"), (1, 64, 32, "z"), (1, 96, 32, "x")),
 )
@@ -81,9 +81,9 @@
 def kernel(
     sizes, amp_ref, left_hbm, right_hbm, out_ref,
     left_buf, left_f32, right_buf, right_f32, own, got, halved, prod, core_got, chip, z_got,
-    z_total, x_got, x_total, last_got,
+    z_total, x_got, x_total, last_got, out_buf,
     load_sem, right_sem, ag_send, ag_recv, core_send, core_recv, z_send, z_recv, x_send, x_recv,
-    last_send, last_recv,
+    last_send, last_recv, out_sem,
 ):
     pairs, d_block, c_block, vectors, width = sizes
     depth = d_block * vectors
@@ -381,6 +381,10 @@
     own_tile = 2 * (x // 2) + c
     own_offset = lax.rem(own_tile - y + 4, 4)
 
+    def out_copy(part):
+        span = pl.ds(part.tile_row, part.rows)
+        return pltpu.make_async_copy(out_buf.at[span, :], out_ref.at[span, :], out_sem)
+
     def final(g):
         for part in PARTS:
             if part.group != g:
@@ -399,7 +403,9 @@
                     total = last_got[0, at, :].astype(F32)
                     for k in range(1, 4):
                         total = total + last_got[k, at, :].astype(F32)
-                    out_ref[at, :] = total
+                    out_buf[at, :] = total
+
+                out_copy(part).start()
 
     def gathered(g):
         k = g - GATHERED
@@ -416,6 +422,7 @@
     for way in range(2):
         landed(got.at[pl.ds(0, (ROWS - width) // 2), :], ag_send.at[way])
     landed(z_got, z_send)
+    landed(out_buf, out_sem)
     for part in PARTS:
         if part.first == "z":
             wait_last(part)
@@ -445,7 +452,7 @@
             pl.BlockSpec(memory_space=pl.ANY),
             pl.BlockSpec(memory_space=pl.ANY),
         ],
-        out_specs=pl.BlockSpec(memory_space=pltpu.VMEM),
+        out_specs=pl.BlockSpec(memory_space=pl.ANY),
         scratch_shapes=[
             pltpu.VMEM((2, c_block, PB, width), BF16),
             pltpu.VMEM((width // 128, c_block * PB, 128), F32),
@@ -462,6 +469,7 @@
             pltpu.VMEM((3, pairs // 2, ROWS_X, width), BF16),
             pltpu.VMEM((pairs // 2, ROWS_X, width), BF16),
             pltpu.VMEM((4, width, width), BF16),
+            pltpu.VMEM((width, width), F32),
             dma((2,)),
             dma((width // CH,)),
             dma((2,)),
@@ -474,6 +482,7 @@
             dma((NG,)),
             dma((len(PARTS),)),
             dma((len(PARTS),)),
+            dma,
         ],
         compiler_params=pltpu.CompilerParams(
             collective_id=0, has_side_effects=True, vmem_limit_bytes=67_043_328

time: 84.2 us -> 83.5 us (level)
  no operation moved by 1% of the time
where the time goes in v5:
time: 83.5 us; the launch traced here: 82.9 us
  Pallas kernels  80.8 us (97%)
  local copies, waits for them, and re-layouts  2.11 us (3%)
    pallas_call x1, Pallas kernels, shards(): pl.pallas_call(functools.partial(kernel, (pairs, d_block, c_block, vector...  80.8 us
    broadcast_in_dim x1, local copies, waits for them, and re-layouts, shards(): return turned.T[None]  2.11 us

profile of v5, /device:TPU:1, one launch (start us, length us, event | category | flops | bytes accessed | tf_op | source)
XLA Modules:
  0.0 82.9 jit_solution(5022245010730671780)
XLA Ops:
  0.0 80.8 %shard_map.37 = f32[384,384]{1,0:T(8,128)} custom-call(bf16[128,64]{1,0:T(8,128)(2,1)} %bitcast.5, bf16[64,144,384]{2,1,0:T(8,128)(2,1)} %left_hbm.1, bf16[16,144,384]{2,1,0:T(8,128)(2,1)} %right_hbm.1), custom_call_target="tpu_custom_call" | custom-call | tf_op jit(solution)/shard_map/pallas_call | solution.py:447
  80.8 2.1 %copy.4 = f32[1,384,384]{2,1,0:T(8,128)} copy(f32[1,384,384]{1,2,0:T(8,128)} %bitcast.4) | data formatting | bytes 1179648 | tf_op jit(solution)/shard_map/broadcast_in_dim | solution.py:491

commit v6 on v5

--- a/solution.py
+++ b/solution.py
@@ -22,7 +22,7 @@
     ((0, 256, 128, "z"),),
     ((3, 0, 128, "x"), (1, 256, 128, "x")),
     ((3, 128, 128, "z"), (1, 128, 128, "z")),
-    ((2, 0, 128, "z"), (2, 256, 128, "z")),
+    ((2, 0, 128, "z"), (2, 256, 128, "x")),
     ((2, 128, 64, "z"), (2, 192, 64, "x")),
     ((3, 256, 64, "z"), (1, 0, 64, "z")),
     ((3, 320, 32, "z"), (3, 352, 32, "x"), (1, 64, 32, "z"), (1, 96, 32, "x")),

time: 83.5 us -> 83.9 us (level)
  no operation moved by 1% of the time
where the time goes in v6:
time: 83.9 us; the launch traced here: 83.3 us
  Pallas kernels  81.2 us (97%)
  local copies, waits for them, and re-layouts  2.11 us (3%)
    pallas_call x1, Pallas kernels, shards(): pl.pallas_call(functools.partial(kernel, (pairs, d_block, c_block, vector...  81.2 us
    broadcast_in_dim x1, local copies, waits for them, and re-layouts, shards(): return turned.T[None]  2.11 us

profile of v6, /device:TPU:1, one launch (start us, length us, event | category | flops | bytes accessed | tf_op | source)
XLA Modules:
  0.0 83.3 jit_solution(13957771857571075739)
XLA Ops:
  0.0 81.2 %shard_map.37 = f32[384,384]{1,0:T(8,128)} custom-call(bf16[128,64]{1,0:T(8,128)(2,1)} %bitcast.5, bf16[64,144,384]{2,1,0:T(8,128)(2,1)} %left_hbm.1, bf16[16,144,384]{2,1,0:T(8,128)(2,1)} %right_hbm.1), custom_call_target="tpu_custom_call" | custom-call | tf_op jit(solution)/shard_map/pallas_call | solution.py:447
  81.2 2.1 %copy.4 = f32[1,384,384]{2,1,0:T(8,128)} copy(f32[1,384,384]{1,2,0:T(8,128)} %bitcast.4) | data formatting | bytes 1179648 | tf_op jit(solution)/shard_map/broadcast_in_dim | solution.py:491
